TPU v7x, 32 devices: a whole 2x2x4 slice. The times are simulated.
32 devices in a mesh: feat: 8 (over z, core), node: 4 (over y, x).
Axes of the slice: x: 2, y: 2, z: 4, core: 2. Of those that a mesh axis runs over, the one named last changes fastest.
Arguments:
- node_features: bfloat16 [1024, 4, 1024], P('feat', 'node'), may hold values from -6 to 6
- weight: bfloat16 [1024, 256], P('feat'), may hold values from -0.1875 to 0.1875
- out_bias: float32 [256], replicated, may hold values from -3 to 3
- edge_tiles: bfloat16 [4, 8, 8, 128, 128], P('node', 'feat'), may hold values from 0.049804688 to 1
- tile_column: int32 [4, 8, 8], P('node', 'feat'), may hold values from 0 to 7, as said below
- tile_count: int32 [4, 8], P('node', 'feat'), may hold values from 1 to 8, as said below
- grad_hidden: bfloat16 [4, 1024, 256], P('node', 'feat'), may hold values from -6 to 6
Outputs:
- hidden: bfloat16 [4, 1024, 256], P('node', 'feat')
- grad_features: bfloat16 [1024, 4, 1024], P('feat', 'node')
- weight_grad: float32 [1024, 256], P('feat')
Inputs may be any that keep to these rules, and one draw needn't show every extreme that they name: `tile_column`: the 8 column blocks listed for one row block are distinct, live slots or not. `tile_count`: slots of a row block beyond its count are ignored. In every cluster some row block has exactly 8 live tiles.
All inputs are finite; a program needn't handle non-finite values.
Results may differ from a plain program's by a relative error of at most 0.007.
Values may be sent and summed in bfloat16 or wider, within the bound.
A program may use at most 64 MiB of HBM per device.

v0:
```python
import math
import jax
import jax.numpy as jnp
from jax import lax
from jax.sharding import PartitionSpec as P


def gelu_tanh(pre_value):
    return jax.nn.gelu(pre_value, approximate=True)


def body(node_features, weight, out_bias, edge_tiles, tile_column, tile_count, grad_hidden):
    feat_dev, clusters, cluster_rows = node_features.shape
    blocks = lax.axis_size("feat")
    tile_rows = cluster_rows // blocks
    hidden_width = weight.shape[1]
    summed_rows = lax.psum_scatter(
        jnp.einsum("fqr,fh->rqh", node_features, weight, preferred_element_type=jnp.float32),
        "feat",
        scatter_dimension=0,
        tiled=True,
    )
    own_proj = jnp.transpose(summed_rows, (1, 0, 2))
    own_rounded = own_proj.astype(jnp.bfloat16)
    all_proj = lax.all_gather(own_rounded, "feat", axis=1, tiled=True)
    blocks_proj = all_proj.reshape(clusters, blocks, tile_rows, hidden_width)
    my_tiles = edge_tiles[:, 0]
    my_cols = tile_column[:, 0]
    counts = tile_count[:, 0]
    slot_ids = jnp.arange(my_tiles.shape[1], dtype=jnp.int32)
    live_mask = (slot_ids[None, :] < counts[:, None]).astype(jnp.bfloat16)
    masked = my_tiles * live_mask[:, :, None, None]
    degree = jnp.sum(masked, axis=(1, 3), dtype=jnp.float32)
    cluster_ids = jnp.arange(clusters, dtype=jnp.int32)[:, None]
    chosen = blocks_proj[cluster_ids, my_cols]
    summed = jnp.einsum("qsij,qsjh->qih", masked, chosen, preferred_element_type=jnp.float32)
    row_scale = lax.rsqrt(degree)[:, :, None]
    pre_act = summed * row_scale + out_bias
    activated, backward = jax.vjp(gelu_tanh, pre_act)
    hidden = activated.astype(jnp.bfloat16)
    (grad_pre,) = backward(grad_hidden.astype(jnp.float32))
    scaled = (grad_pre * row_scale).astype(jnp.bfloat16)
    tile_terms = jnp.einsum(
        "qsij,qih->qsjh", masked, scaled, preferred_element_type=jnp.float32
    ).astype(jnp.bfloat16)
    outgoing = (
        jnp.zeros((blocks, clusters, tile_rows, hidden_width), jnp.bfloat16)
        .at[my_cols, cluster_ids]
        .set(tile_terms)
    )
    arrived = lax.all_to_all(outgoing, "feat", split_axis=0, concat_axis=0, tiled=True)
    own_grad = jnp.sum(arrived, axis=0, dtype=jnp.float32).astype(jnp.bfloat16)
    all_grad = lax.all_gather(own_grad, "feat", axis=1, tiled=True)
    grad_features = jnp.einsum(
        "fh,qrh->fqr", weight, all_grad, preferred_element_type=jnp.float32
    ).astype(jnp.bfloat16)
    partial_grad = jnp.einsum(
        "fqr,qrh->fh", node_features, all_grad, preferred_element_type=jnp.float32
    )
    total_nodes = clusters * lax.axis_size("node") * cluster_rows
    weight_grad = lax.psum(partial_grad, "node") * (1.0 / math.sqrt(total_nodes))
    return (hidden, grad_features, weight_grad)


def solution(mesh):
    return jax.shard_map(
        body,
        mesh=mesh,
        in_specs=(
            P("feat", "node", None),
            P("feat", None),
            P(),
            P("node", "feat", None, None, None),
            P("node", "feat", None),
            P("node", "feat"),
            P("node", "feat", None),
        ),
        out_specs=(P("node", "feat", None), P("feat", "node", None), P("feat", None)),
        check_vma=False,
    )
```

profile of v0, /device:TPU:0, one launch (start us, length us, event | category | flops | bytes accessed | tf_op | source)
XLA Modules:
  0.0 150.2 jit_solution(10850708865901555610)
XLA Ops:
  7.2 0.0 copy-start
  7.2 0.0 reduce-scatter.2.cloned.1.call-start
  7.2 0.9 copy-done
  8.1 2.1 %convolution_bitcast_fusion = f32[1024,1,256]{0,2,1:T(8,128)} fusion(bf16[128,256]{1,0:T(8,128)(2,1)} %param.8, bf16[128,1,1024]{2,0,1:T(8,128)(2,1)S(1)} %copy-done), kind=kOutput, calls=%fused_computation.2 | convolution fusion | flops 67108864 | bytes 1376256 | tf_op jit(solution)/shard_map/fqr,fh->rqh/dot_general | solution.py:18
  10.3 0.0 copy-start.1
  10.3 0.0 reduce-scatter.2.cloned.1.call-update
  11.0 0.2 copy-done.1
  11.2 0.2 convert_reduce_fusion
  11.4 0.0 copy-start.5
  11.4 0.6 copy-done.5
  12.1 33.3 %reduce-scatter.2.cloned.1.call-done = f32[128,1,256]{0,2,1:T(8,128)} async-done(((f32[1024,1,256]{0,2,1:T(8,128)}), f32[128,1,256]{0,2,1:T(8,128)}) %reduce-scatter.2.cloned.1.call-update) | async-done | bytes 131088 | tf_op jit(solution)/shard_map/reduce_scatter | solution.py:17
  45.5 0.9 convert_element_type.64
  46.4 14.0 %all-gather = bf16[1024,1,256]{0,2,1:T(8,128)(2,1)S(1)} all-gather(bf16[128,1,256]{0,2,1:T(8,128)(2,1)S(1)} %convert_element_type.64), channel_id=2, replica_groups=mesh['feat'=8,'node'=4] {'feat'}, dimensions={0}, use_global_device_ids=true | all-gather | bytes 589824 | tf_op jit(solution)/shard_map/all_gather | solution.py:25
  60.4 0.2 copy.22
  60.6 0.0 copy-start.3
  60.6 0.6 gather_fusion
  61.2 0.1 copy-done.3
  61.3 0.0 copy-start.4
  61.3 0.3 fusion.2
  61.5 0.6 copy-done.4
  62.1 0.4 convolution_convert_fusion
  62.5 0.8 broadcast.100
  63.4 2.5 %scatter_fusion = bf16[8,128,256]{2,1,0:T(8,128)(2,1)} fusion(bf16[8,128,256]{2,1,0:T(8,128)(2,1)} %broadcast.100, s32[8]{0:T(128)S(1)} %fusion.32, bf16[8,128,256]{2,1,0:T(8,128)(2,1)S(1)} %convolution_convert_fusion), kind=kCustom, calls=%fused_computation.1 | custom fusion | bytes 1572896 | tf_op jit(solution)/shard_map/scatter | solution.py:49
  65.8 3.5 %all-to-all-start = ((bf16[8,1,128,256]{3,2,1,0:T(8,128)(2,1)}), bf16[8,1,128,256]{3,2,1,0:T(8,128)(2,1)S(1)}, u32[]{:S(2)}, u32[]{:S(2)}) async-start(bf16[8,1,128,256]{3,2,1,0:T(8,128)(2,1)} %bitcast.21), calls=%async_computation.1 | async-start | bytes 1048576 | tf_op jit(solution)/shard_map/all_to_all | solution.py:51
  69.3 0.0 all-reduce.4.cloned.1.call-start
  69.4 0.7 fusion.31
  70.0 14.6 %all-to-all-done = bf16[8,1,128,256]{3,2,1,0:T(8,128)(2,1)S(1)} async-done(((bf16[8,1,128,256]{3,2,1,0:T(8,128)(2,1)}), bf16[8,1,128,256]{3,2,1,0:T(8,128)(2,1)S(1)}, u32[]{:S(2)}, u32[]{:S(2)}) %all-to-all-start) | async-done | bytes 524320 | tf_op jit(solution)/shard_map/all_to_all | solution.py:51
  84.6 0.1 reduce_sum.24
  84.7 14.9 %all-gather.1 = bf16[1024,256]{1,0:T(8,128)(2,1)S(1)} all-gather(bf16[128,256]{1,0:T(8,128)(2,1)S(1)} %reduce_sum.24), channel_id=3, replica_groups=mesh['feat'=8,'node'=4] {'feat'}, dimensions={0}, use_global_device_ids=true | all-gather | bytes 589824 | tf_op jit(solution)/shard_map/all_gather | solution.py:53
  99.6 1.0 convolution_bitcast_fusion.1
  100.6 0.0 copy-start.2
  100.6 0.0 all-reduce.4.cloned.1.call-update
  100.6 0.8 copy-done.2
  101.5 0.3 fusion
  101.8 0.9 copy.19
  102.6 39.1 %all-reduce.4.cloned.1.call-done = f32[128,256]{0,1:T(8,128)} async-done(((f32[128,256]{0,1:T(8,128)}), f32[128,256]{0,1:T(8,128)}) %all-reduce.4.cloned.1.call-update) | async-done | bytes 131088 | tf_op jit(solution)/shard_map/psum | solution.py:61
  141.7 0.9 broadcast_multiply_fusion
  142.6 0.8 copy.20
  (6 shorter events, 0.0 us)
Async XLA Ops:
  7.2 1.0 copy-start
  7.2 38.3 %reduce-scatter.2.cloned.1.call-start = ((), (), s32[]{:S(2)}) async-start(), calls=%async_computation.2 | async-start | bytes 1179648 | tf_op jit(solution)/shard_map/reduce_scatter | solution.py:17
  10.3 1.0 copy-start.1
  11.4 0.7 copy-start.5
  60.6 0.7 copy-start.3
  61.3 0.8 copy-start.4
  65.8 18.8 %all-to-all-start = ((bf16[8,1,128,256]{3,2,1,0:T(8,128)(2,1)}), bf16[8,1,128,256]{3,2,1,0:T(8,128)(2,1)S(1)}, u32[]{:S(2)}, u32[]{:S(2)}) async-start(bf16[8,1,128,256]{3,2,1,0:T(8,128)(2,1)} %bitcast.21), calls=%async_computation.1 | async-start | bytes 1048576 | tf_op jit(solution)/shard_map/all_to_all | solution.py:51
  69.3 72.4 %all-reduce.4.cloned.1.call-start = ((), (), s32[]{:S(2)}) async-start(), calls=%async_computation.3 | async-start | bytes 262144 | tf_op jit(solution)/shard_map/psum | solution.py:61
  100.6 0.8 copy-start.2
Sparse Core Ops, SparseCore 0:
  10.4 35.0 reduce-scatter.1
  100.8 40.8 all-reduce.3
where the time goes:
time: 151 us; the launch traced here: 150 us
  waiting for transfers between devices  87 us (58%)
  blocking collectives  28.9 us (19%)
  between operations  14.8 us (10%)
  local copies, waits for them, and re-layouts  8.93 us (6%)
  matrix products  4.12 us (3%)
  starting transfers between devices  3.57 us (2%)
  other arithmetic  2.8 us (2%)
    psum x1, waiting for transfers between devices, body(): lax.psum(partial_grad, 'node') * (1.0 / math.sqrt(total_nodes))  39.1 us
    reduce_scatter x1, waiting for transfers between devices, body(): lax.psum_scatter(jnp.einsum('fqr,fh->rqh', node_features, weight, preferr...  33.3 us
    all_gather x1, blocking collectives, body(): all_grad = lax.all_gather(own_grad, 'feat', axis=1, tiled=True)  14.9 us
    all_to_all x1, waiting for transfers between devices, body(): lax.all_to_all(outgoing, 'feat', split_axis=0, concat_axis=0, tiled=True)  14.6 us
    all_gather x1, blocking collectives, body(): all_proj = lax.all_gather(own_rounded, 'feat', axis=1, tiled=True)  14 us
    unnamed x14, local copies, waits for them, and re-layouts  4.86 us
    all_to_all x1, starting transfers between devices, body(): lax.all_to_all(outgoing, 'feat', split_axis=0, concat_axis=0, tiled=True)  3.49 us
  transfers between devices with their start and end apart: 3, of which 3 were waited for; matrix products, arithmetic and copies ran while one was open for 1% of the time, Pallas kernels for 0%

commit v1 on v0

--- a/solution.py
+++ b/solution.py
@@ -3,6 +3,12 @@
 import jax.numpy as jnp
 from jax import lax
 from jax.sharding import PartitionSpec as P
+
+
+def in_order(blocks, dim):
+    lengths = list(blocks.shape[1:])
+    lengths[dim] *= blocks.shape[0]
+    return jnp.moveaxis(blocks, 0, dim).reshape(lengths)
 
 
 def gelu_tanh(pre_value):
@@ -50,7 +56,19 @@
     )
     arrived = lax.all_to_all(outgoing, "feat", split_axis=0, concat_axis=0, tiled=True)
     own_grad = jnp.sum(arrived, axis=0, dtype=jnp.float32).astype(jnp.bfloat16)
-    all_grad = lax.all_gather(own_grad, "feat", axis=1, tiled=True)
+    size = lax.axis_size("feat")
+    pairs = [(i, (i + 1) % size) for i in range(size)]
+    back = [(b, a) for a, b in pairs]
+    lower, upper = ([], [])
+    for step in range(size - 1):
+        if step % 2 == 0:
+            lower.append(lax.ppermute(lower[-1] if lower else own_grad, "feat", pairs))
+        else:
+            upper.append(lax.ppermute(upper[-1] if upper else own_grad, "feat", back))
+    tiles = jnp.stack([*lower[::-1], own_grad, *upper])
+    shift = lax.axis_index("feat") - len(lower)
+    tiles = tiles[(jnp.arange(size) - shift) % size]
+    all_grad = in_order(tiles, 1)
     grad_features = jnp.einsum(
         "fh,qrh->fqr", weight, all_grad, preferred_element_type=jnp.float32
     ).astype(jnp.bfloat16)

time: 151 us -> 158 us (1.046)
  starting transfers between devices: 3.57 us -> 10.9 us
  blocking collectives: 28.9 us -> 31.8 us
  local copies, waits for them, and re-layouts: 8.93 us -> 7.05 us
    all_to_all x0 -> x1, blocking collectives: none -> 17.8 us  [body(): lax.all_to_all(outgoing, 'feat', split_axis=0, concat_axis=0, tiled=True)]
    all_gather x1 -> x0, blocking collectives: 14.9 us -> none  [body(): all_grad = lax.all_gather(own_grad, 'feat', axis=1, tiled=True)]
    all_to_all x1 -> x0, waiting for transfers between devices: 14.6 us -> none  [body(): lax.all_to_all(outgoing, 'feat', split_axis=0, concat_axis=0, tiled=True)]
    ppermute x0 -> x7, waiting for transfers between devices: none -> 11.2 us  [the longest x4 10.6 us: body(): lower.append(lax.ppermute(lower[-1] if lower else own_grad, 'feat', pairs))]
    ppermute x0 -> x7, starting transfers between devices: none -> 10.8 us  [the longest x3 10.7 us: body(): upper.append(lax.ppermute(upper[-1] if upper else own_grad, 'feat', back))]
    all_to_all x1 -> x0, starting transfers between devices: 3.49 us -> none  [body(): lax.all_to_all(outgoing, 'feat', split_axis=0, concat_axis=0, tiled=True)]
    psum x1, waiting for transfers between devices: 39.1 us -> 41.5 us  [body(): lax.psum(partial_grad, 'node') * (1.0 / math.sqrt(total_nodes))]
    scatter x1, local copies, waits for them, and re-layouts: 2.46 us -> 0.78 us  [body(): outgoing = jnp.zeros((blocks, clusters, tile_rows, hidden_width), jnp.bfl...]
  transfers between devices with their start and end apart: 3 -> 9, of which waited for: 3 -> 7; matrix products, arithmetic and copies ran while one was open for 1% -> 1% of each run, Pallas kernels for 0% -> 0%
where the time goes in v1:
time: 158 us
  waiting for transfers between devices  86.1 us (54%)
  blocking collectives  31.8 us (20%)
  between operations  14.9 us (9%)
  starting transfers between devices  10.9 us (7%)
  local copies, waits for them, and re-layouts  7.05 us (4%)
  matrix products  4.12 us (3%)
  other arithmetic  2.82 us (2%)
    psum x1, waiting for transfers between devices, body(): lax.psum(partial_grad, 'node') * (1.0 / math.sqrt(total_nodes))  41.5 us
    reduce_scatter x1, waiting for transfers between devices, body(): lax.psum_scatter(jnp.einsum('fqr,fh->rqh', node_features, weight, preferr...  33.4 us
    all_to_all x1, blocking collectives, body(): lax.all_to_all(outgoing, 'feat', split_axis=0, concat_axis=0, tiled=True)  17.8 us
    all_gather x1, blocking collectives, body(): all_proj = lax.all_gather(own_rounded, 'feat', axis=1, tiled=True)  14 us
    ppermute x3, starting transfers between devices, body(): upper.append(lax.ppermute(upper[-1] if upper else own_grad, 'feat', back))  10.7 us
    ppermute x4, waiting for transfers between devices, body(): lower.append(lax.ppermute(lower[-1] if lower else own_grad, 'feat', pairs))  10.6 us
    unnamed x21, local copies, waits for them, and re-layouts  4.84 us
  transfers between devices with their start and end apart: 9, of which 7 were waited for; matrix products, arithmetic and copies ran while one was open for 1% of the time, Pallas kernels for 0%

profile of v1, /device:TPU:0, one launch (start us, length us, event | category | flops | bytes accessed | tf_op | source)
XLA Modules:
  0.0 157.6 jit_solution(7951356761808314328)
XLA Ops:
  7.2 0.0 copy-start
  7.2 0.0 reduce-scatter.2.cloned.1.call-start
  7.2 0.9 copy-done
  8.1 2.1 %convolution_bitcast_fusion = f32[1024,1,256]{0,2,1:T(8,128)} fusion(bf16[128,256]{1,0:T(8,128)(2,1)} %param.8, bf16[128,1,1024]{2,0,1:T(8,128)(2,1)S(1)} %copy-done), kind=kOutput, calls=%fused_computation.3 | convolution fusion | flops 67108864 | bytes 1376256 | tf_op jit(solution)/shard_map/fqr,fh->rqh/dot_general | solution.py:24
  10.2 0.0 copy-start.1
  10.2 0.0 reduce-scatter.2.cloned.1.call-update
  10.3 0.0 all-reduce.4.cloned.1.call-start
  11.0 0.2 copy-done.1
  11.2 0.2 convert_reduce_fusion
  11.4 0.0 copy-start.5
  11.4 0.6 copy-done.5
  12.1 33.4 %reduce-scatter.2.cloned.1.call-done = f32[128,1,256]{0,2,1:T(8,128)} async-done(((f32[1024,1,256]{0,2,1:T(8,128)}), f32[128,1,256]{0,2,1:T(8,128)}) %reduce-scatter.2.cloned.1.call-update) | async-done | bytes 131088 | tf_op jit(solution)/shard_map/reduce_scatter | solution.py:23
  45.5 0.9 convert_element_type.64
  46.4 14.0 %all-gather = bf16[1024,1,256]{0,2,1:T(8,128)(2,1)S(1)} all-gather(bf16[128,1,256]{0,2,1:T(8,128)(2,1)S(1)} %convert_element_type.64), channel_id=2, replica_groups=mesh['feat'=8,'node'=4] {'feat'}, dimensions={0}, use_global_device_ids=true | all-gather | bytes 589824 | tf_op jit(solution)/shard_map/all_gather | solution.py:31
  60.4 0.2 copy.22
  60.6 0.0 copy-start.3
  60.6 0.6 gather_fusion
  61.2 0.1 copy-done.3
  61.3 0.0 copy-start.4
  61.3 0.3 fusion.2
  61.5 0.6 copy-done.4
  62.1 0.4 convolution_convert_fusion
  62.6 0.8 scatter_fusion
  63.4 17.8 %all_to_all.5 = bf16[8,1,128,256]{3,2,1,0:T(8,128)(2,1)S(1)} all-to-all(bf16[8,1,128,256]{3,2,1,0:T(8,128)(2,1)S(1)} %bitcast.105), channel_id=1, replica_groups=mesh['feat'=8,'node'=4] {'feat'}, dimensions={0} | all-to-all | bytes 1048576 | tf_op jit(solution)/shard_map/all_to_all | solution.py:57
  81.1 0.1 reduce_sum.24
  81.2 0.1 collective-permute-start
  81.3 5.5 %collective-permute-done = bf16[1,128,256]{2,1,0:T(8,128)(2,1)S(1)} collective-permute-done((bf16[1,128,256]{2,1,0:T(8,128)(2,1)S(1)}, bf16[1,128,256]{2,1,0:T(8,128)(2,1)S(1)}, u32[]{:S(2)}, u32[]{:S(2)}) %collective-permute-start) | collective-permute-done | bytes 65568 | tf_op jit(solution)/shard_map/ppermute | solution.py:65
  86.8 0.0 collective-permute-start.1
  86.8 3.6 %collective-permute-start.4 = (bf16[1,128,256]{2,1,0:T(8,128)(2,1)S(1)}, bf16[1,128,256]{2,1,0:T(8,128)(2,1)S(1)}, u32[]{:S(2)}, u32[]{:S(2)}) collective-permute-start(bf16[1,128,256]{2,1,0:T(8,128)(2,1)S(1)} %bitcast.111), channel_id=1, source_target_pairs={{4,0},{8,4},{12,8},{16,12},{20,16},{24,20},{28,24},{0,28},{5,1},{9... | collective-permute-start | bytes 196616 | tf_op jit(solution)/shard_map/ppermute | solution.py:67
  90.4 1.9 %collective-permute-done.1 = bf16[1,128,256]{2,1,0:T(8,128)(2,1)S(1)} collective-permute-done((bf16[1,128,256]{2,1,0:T(8,128)(2,1)S(1)}, bf16[1,128,256]{2,1,0:T(8,128)(2,1)S(1)}, u32[]{:S(2)}, u32[]{:S(2)}) %collective-permute-start.1) | collective-permute-done | bytes 65568 | tf_op jit(solution)/shard_map/ppermute | solution.py:65
  92.3 0.0 collective-permute-start.2
  92.3 0.0 collective-permute-done.4
  92.3 3.6 %collective-permute-start.5 = (bf16[1,128,256]{2,1,0:T(8,128)(2,1)S(1)}, bf16[1,128,256]{2,1,0:T(8,128)(2,1)S(1)}, u32[]{:S(2)}, u32[]{:S(2)}) collective-permute-start(bf16[1,128,256]{2,1,0:T(8,128)(2,1)S(1)} %collective-permute-done.4), channel_id=1, source_target_pairs={{4,0},{8,4},{12,8},{16,12},{20,16},{24,20},{28,24},{0,28},{5,1},{9... | collective-permute-start | bytes 196616 | tf_op jit(solution)/shard_map/ppermute | solution.py:67
  95.9 1.9 %collective-permute-done.2 = bf16[1,128,256]{2,1,0:T(8,128)(2,1)S(1)} collective-permute-done((bf16[1,128,256]{2,1,0:T(8,128)(2,1)S(1)}, bf16[1,128,256]{2,1,0:T(8,128)(2,1)S(1)}, u32[]{:S(2)}, u32[]{:S(2)}) %collective-permute-start.2) | collective-permute-done | bytes 65568 | tf_op jit(solution)/shard_map/ppermute | solution.py:65
  97.8 0.0 collective-permute-start.3
  97.8 0.7 fusion.31
  98.5 0.0 collective-permute-done.5
  98.5 3.5 %collective-permute-start.6 = (bf16[1,128,256]{2,1,0:T(8,128)(2,1)S(1)}, bf16[1,128,256]{2,1,0:T(8,128)(2,1)S(1)}, u32[]{:S(2)}, u32[]{:S(2)}) collective-permute-start(bf16[1,128,256]{2,1,0:T(8,128)(2,1)S(1)} %collective-permute-done.5), channel_id=1, source_target_pairs={{4,0},{8,4},{12,8},{16,12},{20,16},{24,20},{28,24},{0,28},{5,1},{9... | collective-permute-start | bytes 196616 | tf_op jit(solution)/shard_map/ppermute | solution.py:67
  102.1 1.3 collective-permute-done.3
  103.4 0.6 collective-permute-done.6
  104.0 0.6 gather_fusion.1
  104.6 1.0 convolution_bitcast_fusion.1
  105.6 0.0 copy-start.2
  105.6 0.0 all-reduce.4.cloned.1.call-update
  105.6 0.8 copy-done.2
  106.4 0.3 fusion
  106.7 0.9 copy.19
  107.5 41.5 %all-reduce.4.cloned.1.call-done = f32[128,256]{0,1:T(8,128)} async-done(((f32[128,256]{0,1:T(8,128)}), f32[128,256]{0,1:T(8,128)}) %all-reduce.4.cloned.1.call-update) | async-done | bytes 131088 | tf_op jit(solution)/shard_map/psum | solution.py:79
  149.1 0.9 broadcast_multiply_fusion
  150.0 0.8 copy.20
  (17 shorter events, 0.1 us)
Async XLA Ops:
  7.2 1.0 copy-start
  7.2 38.3 %reduce-scatter.2.cloned.1.call-start = ((), (), s32[]{:S(2)}) async-start(), calls=%async_computation.2 | async-start | bytes 1179648 | tf_op jit(solution)/shard_map/reduce_scatter | solution.py:23
  10.2 0.9 copy-start.1
  10.3 138.8 %all-reduce.4.cloned.1.call-start = ((), (), s32[]{:S(2)}) async-start(), calls=%async_computation.3 | async-start | bytes 262144 | tf_op jit(solution)/shard_map/psum | solution.py:79
  11.4 0.7 copy-start.5
  60.6 0.7 copy-start.3
  61.3 0.8 copy-start.4
  81.2 5.5 %collective-permute-start = (bf16[1,128,256]{2,1,0:T(8,128)(2,1)S(1)}, bf16[1,128,256]{2,1,0:T(8,128)(2,1)S(1)}, u32[]{:S(2)}, u32[]{:S(2)}) collective-permute-start(bf16[1,128,256]{2,1,0:T(8,128)(2,1)S(1)} %bitcast.110), channel_id=1, source_target_pairs={{0,4},{4,8},{8,12},{12,16},{16,20},{20,24},{24,28},{28,0},{1,5},{5... | collective-permute-start | bytes 196616 | tf_op jit(solution)/shard_map/ppermute | solution.py:65
  86.8 5.6 %collective-permute-start.1 = (bf16[1,128,256]{2,1,0:T(8,128)(2,1)S(1)}, bf16[1,128,256]{2,1,0:T(8,128)(2,1)S(1)}, u32[]{:S(2)}, u32[]{:S(2)}) collective-permute-start(bf16[1,128,256]{2,1,0:T(8,128)(2,1)S(1)} %collective-permute-done), channel_id=1, source_target_pairs={{0,4},{4,8},{8,12},{12,16},{16,20},{20,24},{24,28},{28,0},{1,5},{5... | collective-permute-start | bytes 196616 | tf_op jit(solution)/shard_map/ppermute | solution.py:65
  86.8 5.6 %collective-permute-start.4 = (bf16[1,128,256]{2,1,0:T(8,128)(2,1)S(1)}, bf16[1,128,256]{2,1,0:T(8,128)(2,1)S(1)}, u32[]{:S(2)}, u32[]{:S(2)}) collective-permute-start(bf16[1,128,256]{2,1,0:T(8,128)(2,1)S(1)} %bitcast.111), channel_id=1, source_target_pairs={{4,0},{8,4},{12,8},{16,12},{20,16},{24,20},{28,24},{0,28},{5,1},{9... | collective-permute-start | bytes 196616 | tf_op jit(solution)/shard_map/ppermute | solution.py:67
  92.3 5.5 %collective-permute-start.2 = (bf16[1,128,256]{2,1,0:T(8,128)(2,1)S(1)}, bf16[1,128,256]{2,1,0:T(8,128)(2,1)S(1)}, u32[]{:S(2)}, u32[]{:S(2)}) collective-permute-start(bf16[1,128,256]{2,1,0:T(8,128)(2,1)S(1)} %collective-permute-done.1), channel_id=1, source_target_pairs={{0,4},{4,8},{8,12},{12,16},{16,20},{20,24},{24,28},{28,0},{1,5},{5... | collective-permute-start | bytes 196616 | tf_op jit(solution)/shard_map/ppermute | solution.py:65
  92.3 6.2 %collective-permute-start.5 = (bf16[1,128,256]{2,1,0:T(8,128)(2,1)S(1)}, bf16[1,128,256]{2,1,0:T(8,128)(2,1)S(1)}, u32[]{:S(2)}, u32[]{:S(2)}) collective-permute-start(bf16[1,128,256]{2,1,0:T(8,128)(2,1)S(1)} %collective-permute-done.4), channel_id=1, source_target_pairs={{4,0},{8,4},{12,8},{16,12},{20,16},{24,20},{28,24},{0,28},{5,1},{9... | collective-permute-start | bytes 196616 | tf_op jit(solution)/shard_map/ppermute | solution.py:67
  97.8 5.5 %collective-permute-start.3 = (bf16[1,128,256]{2,1,0:T(8,128)(2,1)S(1)}, bf16[1,128,256]{2,1,0:T(8,128)(2,1)S(1)}, u32[]{:S(2)}, u32[]{:S(2)}) collective-permute-start(bf16[1,128,256]{2,1,0:T(8,128)(2,1)S(1)} %collective-permute-done.2), channel_id=1, source_target_pairs={{0,4},{4,8},{8,12},{12,16},{16,20},{20,24},{24,28},{28,0},{1,5},{5... | collective-permute-start | bytes 196616 | tf_op jit(solution)/shard_map/ppermute | solution.py:65
  98.5 5.4 %collective-permute-start.6 = (bf16[1,128,256]{2,1,0:T(8,128)(2,1)S(1)}, bf16[1,128,256]{2,1,0:T(8,128)(2,1)S(1)}, u32[]{:S(2)}, u32[]{:S(2)}) collective-permute-start(bf16[1,128,256]{2,1,0:T(8,128)(2,1)S(1)} %collective-permute-done.5), channel_id=1, source_target_pairs={{4,0},{8,4},{12,8},{16,12},{20,16},{24,20},{28,24},{0,28},{5,1},{9... | collective-permute-start | bytes 196616 | tf_op jit(solution)/shard_map/ppermute | solution.py:67
  105.6 0.8 copy-start.2
Sparse Core Ops, SparseCore 0:
  10.4 35.0 reduce-scatter.1
  105.7 43.3 all-reduce.3
